TPU v7x, 512 devices: a whole 4x4x16 slice. The times are simulated.
512 devices in a mesh: dp: 16 (over x_lo, y, core), vocab: 32 (over z, x_hi).
Axes of the slice: x: 4 (x_hi: 2, x_lo: 2; x = x_hi * 2 + x_lo), y: 4, z: 16, core: 2. Of those that a mesh axis runs over, the one named last changes fastest.
Arguments:
- passage_hidden: bfloat16 [2048, 2048], P('dp'), may hold values from -7 to 7
- passage_lengths: int32 [32], P('dp'), may hold values from 16 to 64, as said below
- query_ids: int32 [32, 16], P('dp'), may hold values from 0 to 131071
- query_lengths: int32 [32], P('dp'), may hold values from 4 to 16, as said below
- positives: int32 [32], replicated, may hold values from 0 to 31, each once
- head: bfloat16 [2048, 131072], P('dp', 'vocab'), may hold values from -0.125 to 0.125
- df_prev: float32 [131072], P('vocab'), may hold values from 1 to 4096
Outputs:
- head_grad: float32 [2048, 131072], P('dp', 'vocab')
- scores: float32 [32, 32], replicated
Inputs may be any that keep to these rules, and one draw needn't show every extreme that they name: `passage_lengths`: some passage fills all 64 slots. `query_lengths`: some query fills all 16 slots. `positives`: each passage is the positive of exactly one query.
All inputs are finite; a program needn't handle non-finite values.
Results may differ from a plain program's by a relative error of at most 0.00064.
Values may be sent and summed in bfloat16 or wider, within the bound.
No kernel may reach another device: no remote copies, remote signals or barrier semaphores. Data moves between devices by JAX's collectives and lax.ppermute only.
A program may use at most 64 MiB of HBM per device.

v0:
```python
import jax
import jax.numpy as jnp
from jax import lax
from jax.sharding import PartitionSpec as P

flops_weight = 0.3


def ranking_grad(scores, chosen, query_total):
    columns = scores.shape[1]
    onehot = (jnp.arange(columns, dtype=jnp.int32)[None, :] == chosen[:, None]).astype(jnp.float32)
    own_score = jnp.sum(scores * onehot, axis=1, keepdims=True)
    sigmas = jax.nn.sigmoid(scores - own_score)
    return (sigmas - onehot * jnp.sum(sigmas, axis=1, keepdims=True)) / query_total


def local(passage_hidden, passage_lengths, query_ids, query_lengths, positives, head, df_prev):
    dp_count = lax.axis_size("dp")
    dp_index = lax.axis_index("dp")
    vocab_index = lax.axis_index("vocab")
    width_local = head.shape[1]
    column_count = width_local // dp_count
    head_block = lax.all_to_all(head, "dp", split_axis=1, concat_axis=0, tiled=True)
    hidden_all, passage_sizes, query_tokens, query_sizes = (
        lax.all_gather(passage_hidden, "dp", axis=0, tiled=True),
        lax.all_gather(passage_lengths, "dp", axis=0, tiled=True),
        lax.all_gather(query_ids, "dp", axis=0, tiled=True),
        lax.all_gather(query_lengths, "dp", axis=0, tiled=True),
    )
    passage_count = passage_sizes.shape[0]
    seq_span = hidden_all.shape[0] // passage_count
    logits = jnp.dot(hidden_all, head_block, preferred_element_type=jnp.float32)
    softened = jax.nn.softplus(logits)
    activation = jnp.log1p(softened)
    slope_term = jax.nn.sigmoid(logits) / (1.0 + softened)
    positions = jnp.arange(seq_span, dtype=jnp.int32)
    token_mask = (positions[None, :] < passage_sizes[:, None]).astype(jnp.float32)
    token_weight = token_mask / passage_sizes.astype(jnp.float32)[:, None]
    passage_rep = jnp.sum(
        activation.reshape(passage_count, seq_span, column_count) * token_weight[:, :, None], axis=1
    )
    first_column = dp_index * column_count
    doc_freq = lax.dynamic_slice_in_dim(df_prev, first_column, column_count, 0) + jnp.sum(
        1.0 - jnp.exp(-2.0 * passage_rep), axis=0
    )
    term_weight = jnp.log1p(doc_freq)
    column_ids = (
        vocab_index * width_local + first_column + jnp.arange(column_count, dtype=jnp.int32)
    )
    query_mask = jnp.arange(query_tokens.shape[1], dtype=jnp.int32)[None, :] < query_sizes[:, None]
    matches = (query_tokens[:, :, None] == column_ids[None, None, :]) & query_mask[:, :, None]
    query_bag = jnp.sum(matches.astype(jnp.float32), axis=1)
    partial_scores = jnp.dot(
        query_bag,
        passage_rep.T,
        precision=lax.Precision.HIGHEST,
        preferred_element_type=jnp.float32,
    )
    query_total = positives.shape[0]
    scores = lax.psum(partial_scores, ("dp", "vocab"))
    score_grad = ranking_grad(scores, positives, query_total)
    rep_grad = jnp.dot(
        score_grad.T, query_bag, precision=lax.Precision.HIGHEST, preferred_element_type=jnp.float32
    )
    rep_grad = rep_grad + 2.0 * flops_weight / passage_count * term_weight * jnp.mean(
        passage_rep, axis=0
    )
    logit_grad = (
        (token_weight[:, :, None] * rep_grad[:, None, :]).reshape(logits.shape) * slope_term
    ).astype(jnp.bfloat16)
    grad_block = lax.dot_general(
        hidden_all, logit_grad, (((0,), (0,)), ((), ())), preferred_element_type=jnp.float32
    )
    head_grad = lax.all_to_all(grad_block, "dp", split_axis=0, concat_axis=1, tiled=True)
    return (head_grad, scores)


def solution(mesh):
    return jax.shard_map(
        local,
        mesh=mesh,
        in_specs=(
            P("dp", None),
            P("dp"),
            P("dp", None),
            P("dp"),
            P(),
            P("dp", "vocab"),
            P("vocab"),
        ),
        out_specs=(P("dp", "vocab"), P()),
        check_vma=False,
    )
```

profile of v0, /device:TPU:1, one launch (start us, length us, event | category | flops | bytes accessed | tf_op | source)
XLA Modules:
  0.0 239.4 jit_solution(17797994850727579767)
XLA Ops:
  7.2 0.0 all-gather.3.cloned.1.call-start
  7.2 0.7 all-gather.3.cloned.1.call-update
  7.9 0.0 copy-start.3
  7.9 0.0 copy-start.4
  7.9 0.0 copy-start.1
  7.9 2.3 copy.18
  10.2 10.3 %all-to-all-start = ((bf16[128,16,256]{0,2,1:T(8,128)(2,1)}), bf16[128,16,256]{0,2,1:T(8,128)(2,1)S(1)}, u32[]{:S(2)}, u32[]{:S(2)}) async-start(bf16[128,16,256]{0,2,1:T(8,128)(2,1)} %bitcast.3), calls=%async_computation | async-start | bytes 2097152 | tf_op jit(solution)/shard_map/all_to_all | solution.py:23
  20.5 1.3 dynamic-slice
  22.4 0.0 copy-done.3
  22.4 0.2 dynamic-update-slice
  22.7 0.0 copy-done.4
  22.7 0.2 dynamic-update-slice.1
  22.9 18.3 %all-reduce.2 = (s32[32]{0:T(128)S(1)}, s32[32]{0:T(128)S(1)}) all-reduce(s32[32]{0:T(128)S(1)} %dynamic-update-slice.1, s32[32]{0:T(128)S(1)} %dynamic-update-slice), channel_id=1, replica_groups=mesh['dp'=16,'vocab'=32] {'dp'}, use_global_device_ids=true, to_apply=%add.1 | all-reduce | flops 64 | bytes 512
  41.2 0.1 convert_divide_fusion
  41.3 0.1 div.37
  41.4 0.0 copy-done.1
  41.4 19.2 %all-gather = s32[16,2,16]{2,1,0:T(2,128)S(1)} all-gather(s32[1,2,16]{2,1,0:T(2,128)S(1)} %bitcast.35), channel_id=1, replica_groups=mesh['dp'=16,'vocab'=32] {'dp'}, dimensions={0}, use_global_device_ids=true | all-gather | bytes 2176 | tf_op jit(solution)/shard_map/all_gather | solution.py:27
  60.6 0.1 iota_compare_fusion.2
  60.7 0.3 convert_reduce_fusion
  60.9 0.0 all-to-all-done
  61.0 0.5 copy.19
  61.5 15.2 %all-gather.3.cloned.1.call-done = bf16[2048,2048]{1,0:T(8,128)(2,1)} async-done(((bf16[128,2048]{1,0:T(8,128)(2,1)}), bf16[2048,2048]{1,0:T(8,128)(2,1)}) %all-gather.3.cloned.1.call-update) | async-done | bytes 8388624 | tf_op jit(solution)/shard_map/all_gather | solution.py:25
  76.7 7.4 %multiply_reduce_fusion = (f32[256]{0:T(256)S(1)}, f32[2048,256]{1,0:T(8,128)S(1)}) fusion(f32[2048]{0:T(1024)S(1)} %div.37, bf16[2048,2048]{1,0:T(8,128)(2,1)} %all-gather.3.cloned.1.call-done, bf16[2048,256]{1,0:T(8,128)(2,1)S(1)} %bitcast.33), kind=kOutput, calls=%fused_computation.5 | convolution fusion | flops 2151677696 | bytes 11543552 | tf_op jit(solution)/shard_map/dot_general | solution.py:32
  84.1 0.0 copy-start.2
  84.1 1.9 multiply_reduce_fusion.1
  86.1 0.2 fusion.13
  86.2 105.4 %psum.7 = f32[32,32]{1,0:T(8,128)S(1)} all-reduce(f32[32,32]{1,0:T(8,128)S(1)} %fusion.13), channel_id=1, replica_groups=mesh['dp'=16,'vocab'=32] {'dp','vocab'}, use_global_device_ids=true, to_apply=%region_2.3 | all-reduce | flops 1024 | bytes 8192 | tf_op jit(solution)/shard_map/psum | solution.py:60
  191.6 0.0 copy-done.2
  191.6 0.0 copy-start
  191.6 0.2 select_reduce_fusion
  191.8 0.2 fusion.12
  192.0 0.8 multiply_multiply_fusion
  192.8 0.3 convolution_add_fusion
  193.1 1.7 fusion.1
  194.9 5.7 %convolution_bitcast_fusion = f32[32,16,8,128]{3,2,1,0:T(8,128)S(1)} fusion(bf16[2048,256]{1,0:T(8,128)(2,1)S(1)} %fusion.1, bf16[2048,2048]{1,0:T(8,128)(2,1)} %all-gather.3.cloned.1.call-done), kind=kOutput, calls=%fused_computation.8 | convolution fusion | flops 2147483648 | bytes 11534336 | tf_op jit(solution)/shard_map/dot_general | solution.py:71
  200.6 0.0 copy-done
  200.6 0.2 copy.24
  200.8 30.0 %all_to_all.38 = f32[16,128,256]{1,2,0:T(8,128)S(1)} all-to-all(f32[16,128,256]{1,2,0:T(8,128)S(1)} %bitcast.30), channel_id=1, replica_groups=mesh['dp'=16,'vocab'=32] {'dp'}, dimensions={0} | all-to-all | bytes 4194304 | tf_op jit(solution)/shard_map/all_to_all | solution.py:74
  230.8 1.8 copy.21
  (5 shorter events, 0.0 us)
Async XLA Ops:
  7.2 69.5 %all-gather.3.cloned.1.call-start = ((), (), s32[]{:S(2)}) async-start(), calls=%async_computation.2 | async-start | bytes 8912896 | tf_op jit(solution)/shard_map/all_gather | solution.py:25
  7.9 14.5 %copy-start.3 = (s32[2]{0:T(128)S(1)}, s32[2]{0:T(128)}, u32[]{:S(2)}) copy-start(s32[2]{0:T(128)} %param.8) | copy-start | bytes 28
  7.9 14.8 %copy-start.4 = (s32[2]{0:T(128)S(1)}, s32[2]{0:T(128)}, u32[]{:S(2)}) copy-start(s32[2]{0:T(128)} %param.10) | copy-start | bytes 28
  7.9 33.5 %copy-start.1 = (s32[2,16]{1,0:T(2,128)S(1)}, s32[2,16]{1,0:T(2,128)}, u32[]{:S(2)}) copy-start(s32[2,16]{1,0:T(2,128)} %param.9) | copy-start | bytes 388
  10.2 50.7 %all-to-all-start = ((bf16[128,16,256]{0,2,1:T(8,128)(2,1)}), bf16[128,16,256]{0,2,1:T(8,128)(2,1)S(1)}, u32[]{:S(2)}, u32[]{:S(2)}) async-start(bf16[128,16,256]{0,2,1:T(8,128)(2,1)} %bitcast.3), calls=%async_computation | async-start | bytes 2097152 | tf_op jit(solution)/shard_map/all_to_all | solution.py:23
  84.1 107.6 %copy-start.2 = (s32[32]{0:T(128)S(1)}, s32[32]{0:T(128)}, u32[]{:S(2)}) copy-start(s32[32]{0:T(128)} %param.11) | copy-start | bytes 388
  191.6 9.0 %copy-start = (f32[32,32]{1,0:T(8,128)}, f32[32,32]{1,0:T(8,128)S(1)}, u32[]{:S(2)}) copy-start(f32[32,32]{1,0:T(8,128)S(1)} %psum.7) | copy-start | bytes 12292
Sparse Core Ops, SparseCore 0:
  10.1 66.5 all-gather.2
where the time goes:
time: 240 us; the launch traced here: 239 us
  blocking collectives  173 us (72%)
  waiting for transfers between devices  15.9 us (7%)
  between operations  14.8 us (6%)
  matrix products  13.6 us (6%)
  starting transfers between devices  10.3 us (4%)
  local copies, waits for them, and re-layouts  6.64 us (3%)
  other arithmetic  5.26 us (2%)
    psum x1, blocking collectives, local(): scores = lax.psum(partial_scores, ('dp', 'vocab'))  105 us
    all_to_all x1, blocking collectives, local(): lax.all_to_all(grad_block, 'dp', split_axis=0, concat_axis=1, tiled=True)  30 us
    all_gather x1, blocking collectives, local(): lax.all_gather(query_ids, 'dp', axis=0, tiled=True)  19.2 us
    unnamed x1, blocking collectives  18.3 us
    all_gather x1, waiting for transfers between devices, local(): lax.all_gather(passage_hidden, 'dp', axis=0, tiled=True)  15.2 us
    all_to_all x1, starting transfers between devices, local(): lax.all_to_all(head, 'dp', split_axis=1, concat_axis=0, tiled=True)  10.3 us
    dot_general x1, matrix products, local(): logits = jnp.dot(hidden_all, head_block, preferred_element_type=jnp.float32)  7.39 us
    unnamed x17, local copies, waits for them, and re-layouts  5.83 us
  transfers between devices with their start and end apart: 2, of which 1 were waited for; matrix products, arithmetic and copies ran while one was open for 2% of the time, Pallas kernels for 0%

commit v1 on v0

--- a/solution.py
+++ b/solution.py
@@ -57,7 +57,8 @@
         preferred_element_type=jnp.float32,
     )
     query_total = positives.shape[0]
-    scores = lax.psum(partial_scores, ("dp", "vocab"))
+    row_out = lax.all_gather(partial_scores, ("dp", "vocab"))
+    scores = jnp.sum(row_out, axis=0)
     score_grad = ranking_grad(scores, positives, query_total)
     rep_grad = jnp.dot(
         score_grad.T, query_bag, precision=lax.Precision.HIGHEST, preferred_element_type=jnp.float32

time: 240 us -> 1580 us (6.58)
  waiting for transfers between devices: 15.9 us -> 1450 us
  blocking collectives: 173 us -> 67 us
    all_gather x0 -> x1, waiting for transfers between devices: none -> 1430 us  [local(): row_out = lax.all_gather(partial_scores, ('dp', 'vocab'))]
    psum x1 -> x0, blocking collectives: 105 us -> none  [local(): scores = lax.psum(partial_scores, ('dp', 'vocab'))]
  transfers between devices with their start and end apart: 2 -> 3, of which waited for: 1 -> 2; matrix products, arithmetic and copies ran while one was open for 2% -> 0% of each run, Pallas kernels for 0% -> 0%
where the time goes in v1:
time: 1580 us; the launch traced here: 1570 us
  waiting for transfers between devices  1450 us (92%)
  blocking collectives  67 us (4%)
    all_gather x1, waiting for transfers between devices, local(): row_out = lax.all_gather(partial_scores, ('dp', 'vocab'))  1430 us
  transfers between devices with their start and end apart: 3, of which 2 were waited for; matrix products, arithmetic and copies ran while one was open for 0% of the time, Pallas kernels for 0%

profile of v1, /device:TPU:1, one launch (start us, length us, event | category | flops | bytes accessed | tf_op | source)
XLA Modules:
  0.0 1570.6 jit_solution(8109224878212356220)
XLA Ops:
  7.2 0.0 all-gather.5.cloned.1.call-start
  7.2 0.7 all-gather.5.cloned.1.call-update
  7.9 0.0 copy-start.3
  7.9 0.0 copy-start.4
  7.9 0.0 copy-start.1
  7.9 2.3 copy.18
  10.2 10.3 all-to-all-start
  20.5 0.0 all-gather.7.cloned.1.call-start
  20.5 1.3 dynamic-slice
  22.5 0.0 copy-done.3
  22.5 0.2 dynamic-update-slice.1
  22.7 0.0 copy-done.4
  22.7 0.2 dynamic-update-slice
  22.9 18.3 %all-reduce.2 = (s32[32]{0:T(128)S(1)}, s32[32]{0:T(128)S(1)}) all-reduce(s32[32]{0:T(128)S(1)} %dynamic-update-slice.1, s32[32]{0:T(128)S(1)} %dynamic-update-slice), channel_id=1, replica_groups=mesh['dp'=16,'vocab'=32] {'dp'}, use_global_device_ids=true, to_apply=%add.1 | all-reduce | flops 64 | bytes 512
  41.2 0.1 convert_divide_fusion
  41.3 0.1 div.37
  41.4 0.0 copy-done.1
  41.4 19.2 %all-gather.1 = s32[16,2,16]{2,1,0:T(2,128)S(1)} all-gather(s32[1,2,16]{2,1,0:T(2,128)S(1)} %bitcast.37), channel_id=1, replica_groups=mesh['dp'=16,'vocab'=32] {'dp'}, dimensions={0}, use_global_device_ids=true | all-gather | bytes 2176 | tf_op jit(solution)/shard_map/all_gather | solution.py:27
  60.6 0.1 iota_compare_fusion.2
  60.7 0.3 convert_reduce_fusion
  60.9 0.0 all-to-all-done
  61.0 0.5 copy.19
  61.5 15.2 all-gather.5.cloned.1.call-done
  76.7 7.4 multiply_reduce_fusion
  84.1 1.9 multiply_reduce_fusion.1
  86.0 0.8 fusion.13
  86.8 0.0 all-gather.7.cloned.1.call-update
  86.9 0.8 multiply_multiply_fusion
  87.6 1432.4 %all-gather.7.cloned.1.call-done = f32[16384,32]{1,0:T(8,128)} async-done(((f32[32,32]{1,0:T(8,128)}), f32[16384,32]{1,0:T(8,128)}) %all-gather.7.cloned.1.call-update) | async-done | bytes 2097168 | tf_op jit(solution)/shard_map/all_gather | solution.py:60
  1520.0 0.0 copy-start.2
  1520.0 4.0 reduce_sum.65
  1524.0 0.0 copy-done.2
  1524.1 0.0 copy-start
  1524.1 0.2 select_reduce_fusion
  1524.2 0.2 fusion.12
  1524.4 0.3 convolution_add_fusion
  1524.8 1.7 fusion.1
  1526.5 5.7 convolution_bitcast_fusion
  1532.2 0.0 copy-done
  1532.3 0.2 copy.24
  1532.5 29.5 %all_to_all.38 = f32[16,128,256]{1,2,0:T(8,128)S(1)} all-to-all(f32[16,128,256]{1,2,0:T(8,128)S(1)} %bitcast.32), channel_id=1, replica_groups=mesh['dp'=16,'vocab'=32] {'dp'}, dimensions={0} | all-to-all | bytes 4194304 | tf_op jit(solution)/shard_map/all_to_all | solution.py:75
  1562.0 1.8 copy.21
  (5 shorter events, 0.0 us)
Async XLA Ops:
  7.2 69.5 %all-gather.5.cloned.1.call-start = ((), (), s32[]{:S(2)}) async-start(), calls=%async_computation.2 | async-start | bytes 8912896 | tf_op jit(solution)/shard_map/all_gather | solution.py:25
  7.9 14.6 copy-start.3
  7.9 14.8 copy-start.4
  7.9 33.5 %copy-start.1 = (s32[2,16]{1,0:T(2,128)S(1)}, s32[2,16]{1,0:T(2,128)}, u32[]{:S(2)}) copy-start(s32[2,16]{1,0:T(2,128)} %param.9) | copy-start | bytes 388
  10.2 50.7 %all-to-all-start = ((bf16[128,16,256]{0,2,1:T(8,128)(2,1)}), bf16[128,16,256]{0,2,1:T(8,128)(2,1)S(1)}, u32[]{:S(2)}, u32[]{:S(2)}) async-start(bf16[128,16,256]{0,2,1:T(8,128)(2,1)} %bitcast.3), calls=%async_computation | async-start | bytes 2097152 | tf_op jit(solution)/shard_map/all_to_all | solution.py:23
  20.5 1499.6 %all-gather.7.cloned.1.call-start = ((), (), s32[]{:S(2)}) async-start(), calls=%async_computation.3 | async-start | bytes 8404992 | tf_op jit(solution)/shard_map/all_gather | solution.py:60
  1520.0 4.0 copy-start.2
  1524.1 8.2 copy-start
Sparse Core Ops, SparseCore 0:
  10.1 66.5 all-gather.4
  86.9 1433.0 all-gather.6
